TPU v7x, 256 devices: a whole 4x4x8 slice. The times are simulated.
256 devices in a mesh: tm: 16 (over z, core), row: 16 (over x, y).
Axes of the slice: x: 4, y: 4, z: 8, core: 2. Of those that a mesh axis runs over, the one named last changes fastest.
Arguments:
- prior_ensemble: float32 [128, 128, 4096], P('tm', None, 'row'), may hold values from -6 to 6
- observation_data: float32 [128, 8192], P('tm', 'row'), may hold values from -24 to 24
- inverse_error_spread: float32 [8192], P('row'), may hold values from 0.024902152 to 0.24902152
- anomaly_inflation: float32 [128], P('tm'), may hold values from 1.1 to 1.4
- nonzero_tiles: float32 [64, 8, 128, 128], P('row'), may hold values from -0.1875 to 0.1875
- nonzero_tile_targets: int32 [64, 8], P('row'), may hold values from 0 to 31, as said below
Outputs:
- smoothed_ensemble: float32 [128, 128, 4096], P('tm', None, 'row')
- filtered_ensemble: float32 [128, 128, 4096], P('tm', None, 'row')
Inputs may be any that keep to these rules, and one draw needn't show every extreme that they name: `nonzero_tile_targets`: in each block row the 8 block columns are distinct.
All inputs are finite; a program needn't handle non-finite values. Where the computation divides by a largest or mean magnitude, that divisor is 1e-20 or more.
Results may differ from a plain program's by a relative error of at most 0.0003.
Values sent between devices are 32-bit elements; how exact they have to be, the bound alone decides.
A program may use at most 64 MiB of HBM per device.

v0:
```python
import jax
import jax.numpy as jnp
from jax import lax
from jax.sharding import PartitionSpec as P

NS_ITERS = 8
exact_product = lax.Precision.HIGHEST


def passed_along(shard, axis, by):
    length = lax.axis_size(axis)
    pairs = [(i, i + by) for i in range(length) if 0 <= i + by < length]
    return lax.ppermute(shard, axis, pairs)


def ensemble_transforms(info_matrix, info_vector, anomaly_inflation):
    ensemble_entries = info_matrix.shape[-1]
    identity = jnp.eye(ensemble_entries, dtype=jnp.float32)
    row_bound = jnp.max(jnp.sum(jnp.abs(info_matrix), axis=2), axis=1)
    scaled = info_matrix / row_bound[:, None, None]
    root_iter = scaled
    inv_iter = jnp.broadcast_to(identity, scaled.shape)
    for _ in range(NS_ITERS):
        update = 1.5 * identity - 0.5 * jnp.matmul(inv_iter, root_iter, precision=exact_product)
        root_iter = jnp.matmul(root_iter, update, precision=exact_product)
        inv_iter = jnp.matmul(update, inv_iter, precision=exact_product)
    inverse_root = inv_iter / jnp.sqrt(row_bound)[:, None, None]
    half_weights = jnp.einsum("tab,tb->ta", inverse_root, info_vector, precision=exact_product)
    mean_weights = jnp.einsum("tab,tb->ta", inverse_root, half_weights, precision=exact_product)
    spread_norm = float(ensemble_entries - 1) ** 0.5
    mixing = (
        mean_weights[:, :, None] / spread_norm + anomaly_inflation[:, None, None] * inverse_root
    )
    mixing = mixing - jnp.mean(mixing, axis=1, keepdims=True)
    return mixing + 1.0 / ensemble_entries


def local(
    prior_ensemble,
    observation_data,
    inverse_error_spread,
    anomaly_inflation,
    nonzero_tiles,
    nonzero_tile_targets,
):
    ensemble_entries = prior_ensemble.shape[1]
    block_size = nonzero_tiles.shape[2]
    local_rows = nonzero_tiles.shape[0] * block_size

    def observe_single_time(ensemble_shard):
        whole = lax.all_gather(ensemble_shard, "row", axis=1, tiled=True)
        column_count = whole.shape[1] // block_size
        picked = whole.reshape(ensemble_entries, column_count, block_size)[:, nonzero_tile_targets]
        result = jnp.einsum("mbkj,bkij->mbi", picked, nonzero_tiles, precision=exact_product)
        return result.reshape(ensemble_entries, local_rows)

    predicted_observations = lax.map(observe_single_time, prior_ensemble)
    obs_mean = jnp.mean(predicted_observations, axis=1)
    whitened = (
        (predicted_observations - obs_mean[:, None, :])
        * inverse_error_spread
        / float(ensemble_entries - 1) ** 0.5
    )
    innovation = (observation_data - obs_mean) * inverse_error_spread
    part_matrix = jnp.einsum("tmo,tno->tmn", whitened, whitened, precision=exact_product)
    part_vector = jnp.einsum("tmo,to->tm", whitened, innovation, precision=exact_product)
    info_matrix, info_vector = lax.psum((part_matrix, part_vector), "row")
    identity = jnp.eye(ensemble_entries, dtype=jnp.float32)
    info_matrix = info_matrix + identity
    ensemble_weight_factors = ensemble_transforms(info_matrix, info_vector, anomaly_inflation)
    filtered_ensemble = jnp.einsum(
        "fjn,fjt->fnt", ensemble_weight_factors, prior_ensemble, precision=exact_product
    )

    def backward(running, transform):
        product = jnp.matmul(transform, running, precision=exact_product)
        return (product, product)

    _, local_trailing_sum = lax.scan(backward, identity, ensemble_weight_factors, reverse=True)
    shard_product = local_trailing_sum[0]
    final_index = lax.axis_size("tm") - 1
    position = lax.axis_index("tm")

    def one_hop(turn_index, current):
        outgoing = jnp.matmul(shard_product, current, precision=exact_product)
        received = passed_along(outgoing, "tm", -1)
        return jnp.where(position == final_index, identity, received)

    trailing_sum_end = lax.fori_loop(0, final_index, one_hop, identity)
    suffix_product = jnp.einsum(
        "jmk,kl->jml", local_trailing_sum, trailing_sum_end, precision=exact_product
    )
    smoothed_ensemble = jnp.einsum(
        "fjn,fjt->fnt", suffix_product, prior_ensemble, precision=exact_product
    )
    return (smoothed_ensemble, filtered_ensemble)


def solution(mesh):
    placed = (
        P("tm", None, "row"),
        P("tm", "row"),
        P("row"),
        P("tm"),
        P("row", None, None, None),
        P("row", None),
    )
    return jax.shard_map(
        local,
        mesh=mesh,
        in_specs=placed,
        out_specs=(P("tm", None, "row"), P("tm", None, "row")),
        check_vma=False,
    )
```

profile of v0, /device:TPU:97, one launch (start us, length us, event | category | flops | bytes accessed | tf_op | source)
XLA Modules:
  0.0 752.3 jit_solution(10505249584035878029)
XLA Ops:
  8.0 500.9 %while.39 = (s32[]{:T(128)}, f32[8,128,512]{1,2,0:T(8,128)}, f32[8,128,256]{2,1,0:T(8,128)}, s32[4,8]{1,0:T(4,128)}, f32[4,8,128,128]{3,2,1,0:T(8,128)}, /*index=5*/s32[]{:T(128)}) while((s32[]{:T(128)}, f32[8,128,512]{1,2,0:T(8,128)}, f32[8,128,256]{2,1,0:T(8,128)}, s32[4,8]{1,0:T(4,128)}, f32[4,8,128,128]{3,2,1,0:T(8,128)}, ...), condition=%wide.region_1.2_spmd, body=%wide.region_0.1_spmd.sunk | while | flops 805307520 | bytes 20583292 | solution.py:57
  10.6 52.6 %all-gather.5.cloned.1.call-done = f32[1,128,4096]{1,2,0:T(8,128)} async-done(((f32[1,128,256]{1,2,0:T(8,128)}), f32[1,128,4096]{1,2,0:T(8,128)}) %all-gather.5.cloned.1.call-update) | async-done | bytes 2097168 | tf_op jit(solution)/shard_map/while/body/eval_jaxpr/all_gather | solution.py:51
  63.2 1.9 copy.44
  65.1 2.0 gather_fusion
  67.1 4.3 fusion.116
  74.7 51.0 %all-gather.5.cloned.1.call-done = f32[1,128,4096]{1,2,0:T(8,128)} async-done(((f32[1,128,256]{1,2,0:T(8,128)}), f32[1,128,4096]{1,2,0:T(8,128)}) %all-gather.5.cloned.1.call-update) | async-done | bytes 2097168 | tf_op jit(solution)/shard_map/while/body/eval_jaxpr/all_gather | solution.py:51
  127.6 2.0 gather_fusion
  129.6 4.3 fusion.116
  137.2 51.0 %all-gather.5.cloned.1.call-done = f32[1,128,4096]{1,2,0:T(8,128)} async-done(((f32[1,128,256]{1,2,0:T(8,128)}), f32[1,128,4096]{1,2,0:T(8,128)}) %all-gather.5.cloned.1.call-update) | async-done | bytes 2097168 | tf_op jit(solution)/shard_map/while/body/eval_jaxpr/all_gather | solution.py:51
  190.1 2.0 gather_fusion
  192.1 4.3 fusion.116
  199.7 50.7 %all-gather.5.cloned.1.call-done = f32[1,128,4096]{1,2,0:T(8,128)} async-done(((f32[1,128,256]{1,2,0:T(8,128)}), f32[1,128,4096]{1,2,0:T(8,128)}) %all-gather.5.cloned.1.call-update) | async-done | bytes 2097168 | tf_op jit(solution)/shard_map/while/body/eval_jaxpr/all_gather | solution.py:51
  252.3 2.0 gather_fusion
  254.3 4.3 fusion.116
  261.9 50.7 %all-gather.5.cloned.1.call-done = f32[1,128,4096]{1,2,0:T(8,128)} async-done(((f32[1,128,256]{1,2,0:T(8,128)}), f32[1,128,4096]{1,2,0:T(8,128)}) %all-gather.5.cloned.1.call-update) | async-done | bytes 2097168 | tf_op jit(solution)/shard_map/while/body/eval_jaxpr/all_gather | solution.py:51
  314.5 2.0 gather_fusion
  316.5 4.3 fusion.116
  324.1 50.7 %all-gather.5.cloned.1.call-done = f32[1,128,4096]{1,2,0:T(8,128)} async-done(((f32[1,128,256]{1,2,0:T(8,128)}), f32[1,128,4096]{1,2,0:T(8,128)}) %all-gather.5.cloned.1.call-update) | async-done | bytes 2097168 | tf_op jit(solution)/shard_map/while/body/eval_jaxpr/all_gather | solution.py:51
  376.7 2.0 gather_fusion
  378.7 4.3 fusion.116
  386.3 51.0 %all-gather.5.cloned.1.call-done = f32[1,128,4096]{1,2,0:T(8,128)} async-done(((f32[1,128,256]{1,2,0:T(8,128)}), f32[1,128,4096]{1,2,0:T(8,128)}) %all-gather.5.cloned.1.call-update) | async-done | bytes 2097168 | tf_op jit(solution)/shard_map/while/body/eval_jaxpr/all_gather | solution.py:51
  439.3 2.0 gather_fusion
  441.3 4.3 fusion.116
  448.8 51.0 %all-gather.5.cloned.1.call-done = f32[1,128,4096]{1,2,0:T(8,128)} async-done(((f32[1,128,256]{1,2,0:T(8,128)}), f32[1,128,4096]{1,2,0:T(8,128)}) %all-gather.5.cloned.1.call-update) | async-done | bytes 2097168 | tf_op jit(solution)/shard_map/while/body/eval_jaxpr/all_gather | solution.py:51
  501.8 2.0 gather_fusion
  503.8 4.3 fusion.116
  508.9 2.3 reduce_sum.27
  511.3 5.6 fusion.7
  518.5 31.1 %psum.15 = f32[8,128]{1,0:T(8,128)S(1)} all-reduce(f32[8,128]{1,0:T(8,128)S(1)} %bitcast.123), channel_id=1, replica_groups=mesh['tm'=16,'row'=16] {'row'}, use_global_device_ids=true, to_apply=%region_6.7 | all-reduce | flops 1024 | bytes 8192 | tf_op jit(solution)/shard_map/psum | solution.py:67
  549.6 60.8 %all-reduce.2.cloned.1.call-done = f32[8,128,128]{2,1,0:T(8,128)} async-done(((f32[8,128,128]{2,1,0:T(8,128)}), f32[8,128,128]{2,1,0:T(8,128)}) %all-reduce.2.cloned.1.call-update) | async-done | bytes 524304 | tf_op jit(solution)/shard_map/psum | solution.py:67
  630.6 2.0 fusion.50
  632.7 2.0 while.40
  634.7 107.5 %while.41 = (s32[]{:T(128)}, f32[128,128]{1,0:T(8,128)S(1)}, pred[]{:T(512)}, f32[128,128]{1,0:T(8,128)S(1)}, s32[]{:T(128)}) while((s32[]{:T(128)}, f32[128,128]{1,0:T(8,128)S(1)}, pred[]{:T(512)}, f32[128,128]{1,0:T(8,128)S(1)}, s32[]{:T(128)}) %tuple.93), condition=%wide.region_11.12_spmd.clone, body=%wide.region_10.11_spmd.clone.sunk | while | flops 25214976 | bytes 589926 | solution.py:89
  634.9 4.4 collective-permute-start
  639.4 4.3 collective-permute-done
  643.9 1.9 collective-permute-start
  645.8 4.9 collective-permute-done
  650.9 1.9 collective-permute-start
  652.9 4.9 collective-permute-done
  658.0 1.9 collective-permute-start
  659.9 4.9 collective-permute-done
  665.0 1.9 collective-permute-start
  666.9 4.9 collective-permute-done
  672.1 1.9 collective-permute-start
  674.0 4.9 collective-permute-done
  679.1 1.9 collective-permute-start
  681.0 4.9 collective-permute-done
  686.1 1.9 collective-permute-start
  688.1 4.9 collective-permute-done
  693.2 1.9 collective-permute-start
  695.1 4.9 collective-permute-done
  700.2 1.9 collective-permute-start
  702.1 4.9 collective-permute-done
  707.2 1.9 collective-permute-start
  709.2 4.9 collective-permute-done
  714.3 1.9 collective-permute-start
  716.2 4.9 collective-permute-done
  721.3 1.9 collective-permute-start
  723.2 4.9 collective-permute-done
  728.4 1.9 collective-permute-start
  730.3 4.9 collective-permute-done
  735.4 1.9 collective-permute-start
  737.3 4.9 collective-permute-done
  742.8 2.0 fusion.49
  (177 shorter events, 66.2 us)
Async XLA Ops:
  8.0 55.2 %all-gather.5.cloned.1.call-start = ((), (), s32[]{:S(2)}) async-start(), calls=%async_computation.1 | async-start | bytes 2228224 | tf_op jit(solution)/shard_map/while/body/eval_jaxpr/all_gather | solution.py:51
  72.2 53.5 %all-gather.5.cloned.1.call-start = ((), (), s32[]{:S(2)}) async-start(), calls=%async_computation.1 | async-start | bytes 2228224 | tf_op jit(solution)/shard_map/while/body/eval_jaxpr/all_gather | solution.py:51
  134.7 53.5 %all-gather.5.cloned.1.call-start = ((), (), s32[]{:S(2)}) async-start(), calls=%async_computation.1 | async-start | bytes 2228224 | tf_op jit(solution)/shard_map/while/body/eval_jaxpr/all_gather | solution.py:51
  197.2 53.2 %all-gather.5.cloned.1.call-start = ((), (), s32[]{:S(2)}) async-start(), calls=%async_computation.1 | async-start | bytes 2228224 | tf_op jit(solution)/shard_map/while/body/eval_jaxpr/all_gather | solution.py:51
  259.4 53.2 %all-gather.5.cloned.1.call-start = ((), (), s32[]{:S(2)}) async-start(), calls=%async_computation.1 | async-start | bytes 2228224 | tf_op jit(solution)/shard_map/while/body/eval_jaxpr/all_gather | solution.py:51
  321.6 53.2 %all-gather.5.cloned.1.call-start = ((), (), s32[]{:S(2)}) async-start(), calls=%async_computation.1 | async-start | bytes 2228224 | tf_op jit(solution)/shard_map/while/body/eval_jaxpr/all_gather | solution.py:51
  383.8 53.5 %all-gather.5.cloned.1.call-start = ((), (), s32[]{:S(2)}) async-start(), calls=%async_computation.1 | async-start | bytes 2228224 | tf_op jit(solution)/shard_map/while/body/eval_jaxpr/all_gather | solution.py:51
  446.3 53.5 %all-gather.5.cloned.1.call-start = ((), (), s32[]{:S(2)}) async-start(), calls=%async_computation.1 | async-start | bytes 2228224 | tf_op jit(solution)/shard_map/while/body/eval_jaxpr/all_gather | solution.py:51
  508.9 2.4 copy-start.6
  508.9 2.4 copy-start.7
  508.9 2.4 copy-start
  508.9 101.5 %all-reduce.2.cloned.1.call-start = ((), (), s32[]{:S(2)}) async-start(), calls=%async_computation | async-start | bytes 1048576 | tf_op jit(solution)/shard_map/psum | solution.py:67
  517.0 97.2 %copy-start.2 = (f32[128,128]{1,0:T(8,128)}, f32[128,128]{1,0:T(8,128)S(1)}, u32[]{:S(2)}) copy-start(f32[128,128]{1,0:T(8,128)S(1)} %fusion.29) | copy-start | bytes 196612
  610.4 3.8 copy-start.5
  626.9 3.2 copy-start.8
  627.6 3.0 copy-start.1
  630.4 2.3 copy-start.4
  630.6 4.1 copy-start.3
  634.9 8.8 %collective-permute-start = (f32[128,128]{1,0:T(8,128)S(1)}, f32[128,128]{1,0:T(8,128)S(1)}, u32[]{:S(2)}, u32[]{:S(2)}) collective-permute-start(f32[128,128]{1,0:T(8,128)S(1)} %fusion.120), channel_id=1, source_target_pairs={{16,0},{32,16},{48,32},{64,48},{80,64},{96,80},{112,96},{128,112},... | collective-permute-start | bytes 196616 | tf_op jit(solution)/shard_map/while/body/eval_jaxpr/ppermute | solution.py:13
  643.9 6.8 collective-permute-start
  650.9 6.8 collective-permute-start
  658.0 6.8 collective-permute-start
  665.0 6.8 collective-permute-start
  672.1 6.8 collective-permute-start
  679.1 6.8 collective-permute-start
  686.1 6.8 collective-permute-start
  693.2 6.8 collective-permute-start
  700.2 6.8 collective-permute-start
  707.2 6.8 collective-permute-start
  714.3 6.8 collective-permute-start
  721.3 6.8 collective-permute-start
  728.4 6.8 collective-permute-start
  735.4 6.8 collective-permute-start
Sparse Core Ops, SparseCore 0:
  12.2 50.9 all-gather.4
  76.3 49.3 all-gather.4
  138.8 49.3 all-gather.4
  201.0 49.3 all-gather.4
  263.2 49.3 all-gather.4
  325.4 49.3 all-gather.4
  387.9 49.3 all-gather.4
  450.5 49.3 all-gather.4
Sparse Core Ops, SparseCore 1:
  517.0 93.3 all-reduce.1
where the time goes:
time: 753 us; the launch traced here: 752 us
  waiting for transfers between devices  542 us (72%)
  matrix products  69.3 us (9%)
  local copies, waits for them, and re-layouts  51.2 us (7%)
  starting transfers between devices  31.4 us (4%)
  blocking collectives  31.1 us (4%)
  between operations  15.9 us (2%)
  other arithmetic  10 us (1%)
    all_gather x8, waiting for transfers between devices, observe_single_time(): whole = lax.all_gather(ensemble_shard, 'row', axis=1, tiled=True)  409 us
    ppermute x15, waiting for transfers between devices, passed_along(): return lax.ppermute(shard, axis, pairs)  72.4 us
    psum x1, waiting for transfers between devices, local(): info_matrix, info_vector = lax.psum((part_matrix, part_vector), 'row')  60.8 us
    dot_general x8, matrix products, observe_single_time(): jnp.einsum('mbkj,bkij->mbi', picked, nonzero_tiles, precision=exact_product)  34.8 us
    ppermute x15, starting transfers between devices, passed_along(): return lax.ppermute(shard, axis, pairs)  31.3 us
    psum x1, blocking collectives, local(): info_matrix, info_vector = lax.psum((part_matrix, part_vector), 'row')  31.1 us
    gather x8, local copies, waits for them, and re-layouts, observe_single_time(): whole.reshape(ensemble_entries, column_count, block_size)  15.9 us
    reshape x8, local copies, waits for them, and re-layouts, observe_single_time(): whole.reshape(ensemble_entries, column_count, block_size)  15.3 us
  transfers between devices with their start and end apart: 24, of which 24 were waited for; matrix products, arithmetic and copies ran while one was open for 1% of the time, Pallas kernels for 0%

commit v1 on v0

--- a/solution.py
+++ b/solution.py
@@ -48,7 +48,15 @@
     local_rows = nonzero_tiles.shape[0] * block_size
 
     def observe_single_time(ensemble_shard):
-        whole = lax.all_gather(ensemble_shard, "row", axis=1, tiled=True)
+        whole = jnp.concatenate(
+            lax.all_to_all(
+                jnp.stack([ensemble_shard for _ in range(lax.axis_size("row"))], 0),
+                axis_name="row",
+                split_axis=0,
+                concat_axis=0,
+            ),
+            1,
+        )
         column_count = whole.shape[1] // block_size
         picked = whole.reshape(ensemble_entries, column_count, block_size)[:, nonzero_tile_targets]
         result = jnp.einsum("mbkj,bkij->mbi", picked, nonzero_tiles, precision=exact_product)

time: 753 us -> 602 us (0.80)
  waiting for transfers between devices: 542 us -> 340 us
  starting transfers between devices: 31.4 us -> 84 us
  local copies, waits for them, and re-layouts: 51.2 us -> 59.5 us
    all_gather x8 -> x0, waiting for transfers between devices: 409 us -> none  [observe_single_time(): whole = lax.all_gather(ensemble_shard, 'row', axis=1, tiled=True)]
    all_to_all x0 -> x8, waiting for transfers between devices: none -> 203 us  [observe_single_time(): lax.all_to_all(jnp.stack([ensemble_shard for _ in range(lax.axis_size('ro...]
    all_to_all x0 -> x8, starting transfers between devices: none -> 53.2 us  [observe_single_time(): lax.all_to_all(jnp.stack([ensemble_shard for _ in range(lax.axis_size('ro...]
    another operation x0 -> x8, local copies, waits for them, and re-layouts: none -> 12.2 us  [observe_single_time(): jnp.stack([ensemble_shard for _ in range(lax.axis_size('row'))], 0)]
  transfers between devices with their start and end apart: 24 -> 24, of which waited for: 24 -> 24; matrix products, arithmetic and copies ran while one was open for 1% -> 0% of each run, Pallas kernels for 0% -> 0%
where the time goes in v1:
time: 602 us; the launch traced here: 600 us
  waiting for transfers between devices  340 us (56%)
  starting transfers between devices  84 us (14%)
  matrix products  64.3 us (11%)
  local copies, waits for them, and re-layouts  59.5 us (10%)
  blocking collectives  32.5 us (5%)
  between operations  14.4 us (2%)
    all_to_all x8, waiting for transfers between devices, observe_single_time(): lax.all_to_all(jnp.stack([ensemble_shard for _ in range(lax.axis_size('ro...  203 us
    ppermute x15, waiting for transfers between devices, passed_along(): return lax.ppermute(shard, axis, pairs)  72.4 us
    psum x1, waiting for transfers between devices, local(): info_matrix, info_vector = lax.psum((part_matrix, part_vector), 'row')  64.5 us
    all_to_all x8, starting transfers between devices, observe_single_time(): lax.all_to_all(jnp.stack([ensemble_shard for _ in range(lax.axis_size('ro...  53.2 us
    psum x1, blocking collectives, local(): info_matrix, info_vector = lax.psum((part_matrix, part_vector), 'row')  32.5 us
    ppermute x15, starting transfers between devices, passed_along(): return lax.ppermute(shard, axis, pairs)  30.8 us
    dot_general x8, matrix products, observe_single_time(): jnp.einsum('mbkj,bkij->mbi', picked, nonzero_tiles, precision=exact_product)  29.8 us
    gather x8, local copies, waits for them, and re-layouts, observe_single_time(): whole.reshape(ensemble_entries, column_count, block_size)  18.2 us
  transfers between devices with their start and end apart: 24, of which 24 were waited for; matrix products, arithmetic and copies ran while one was open for 0% of the time, Pallas kernels for 0%

profile of v1, /device:TPU:97, one launch (start us, length us, event | category | flops | bytes accessed | tf_op | source)
XLA Modules:
  0.0 600.4 jit_solution(1152252167133277179)
XLA Ops:
  7.2 345.9 %while.39 = (s32[]{:T(128)}, f32[8,128,512]{1,2,0:T(8,128)}, f32[8,128,256]{2,1,0:T(8,128)}, s32[4,8]{1,0:T(4,128)}, f32[4,8,128,128]{3,2,1,0:T(8,128)}, /*index=5*/s32[]{:T(128)}) while((s32[]{:T(128)}, f32[8,128,512]{1,2,0:T(8,128)}, f32[8,128,256]{2,1,0:T(8,128)}, s32[4,8]{1,0:T(4,128)}, f32[4,8,128,128]{3,2,1,0:T(8,128)}, ...), condition=%wide.region_1.2_spmd, body=%wide.region_0.1_spmd.sunk | while | flops 805307520 | bytes 22418832 | solution.py:65
  9.8 6.9 %all-to-all-start = ((f32[16,128,256]{1,2,0:T(8,128)}), f32[16,128,256]{1,2,0:T(8,128)S(1)}, u32[]{:S(2)}, u32[]{:S(2)}) async-start(f32[16,128,256]{1,2,0:T(8,128)} %stack.3), calls=%async_computation | async-start | bytes 4194304 | tf_op jit(solution)/shard_map/while/body/eval_jaxpr/all_to_all | solution.py:52
  16.8 27.8 %all-to-all-done = f32[16,128,256]{1,2,0:T(8,128)S(1)} async-done(((f32[16,128,256]{1,2,0:T(8,128)}), f32[16,128,256]{1,2,0:T(8,128)S(1)}, u32[]{:S(2)}, u32[]{:S(2)}) %all-to-all-start) | async-done | bytes 2097184 | tf_op jit(solution)/shard_map/while/body/eval_jaxpr/all_to_all | solution.py:52
  46.4 2.3 gather_fusion
  48.6 3.7 fusion.116
  55.6 4.0 all-to-all-start
  59.8 25.1 %all-to-all-done = f32[16,128,256]{1,2,0:T(8,128)S(1)} async-done(((f32[16,128,256]{1,2,0:T(8,128)}), f32[16,128,256]{1,2,0:T(8,128)S(1)}, u32[]{:S(2)}, u32[]{:S(2)}) %all-to-all-start) | async-done | bytes 2097184 | tf_op jit(solution)/shard_map/while/body/eval_jaxpr/all_to_all | solution.py:52
  86.7 2.3 gather_fusion
  89.0 3.7 fusion.116
  96.0 6.9 %all-to-all-start = ((f32[16,128,256]{1,2,0:T(8,128)}), f32[16,128,256]{1,2,0:T(8,128)S(1)}, u32[]{:S(2)}, u32[]{:S(2)}) async-start(f32[16,128,256]{1,2,0:T(8,128)} %stack.3), calls=%async_computation | async-start | bytes 4194304 | tf_op jit(solution)/shard_map/while/body/eval_jaxpr/all_to_all | solution.py:52
  103.0 25.0 %all-to-all-done = f32[16,128,256]{1,2,0:T(8,128)S(1)} async-done(((f32[16,128,256]{1,2,0:T(8,128)}), f32[16,128,256]{1,2,0:T(8,128)S(1)}, u32[]{:S(2)}, u32[]{:S(2)}) %all-to-all-start) | async-done | bytes 2097184 | tf_op jit(solution)/shard_map/while/body/eval_jaxpr/all_to_all | solution.py:52
  129.8 2.3 gather_fusion
  132.0 3.7 fusion.116
  139.0 7.1 %all-to-all-start = ((f32[16,128,256]{1,2,0:T(8,128)}), f32[16,128,256]{1,2,0:T(8,128)S(1)}, u32[]{:S(2)}, u32[]{:S(2)}) async-start(f32[16,128,256]{1,2,0:T(8,128)} %stack.3), calls=%async_computation | async-start | bytes 4194304 | tf_op jit(solution)/shard_map/while/body/eval_jaxpr/all_to_all | solution.py:52
  146.3 25.0 %all-to-all-done = f32[16,128,256]{1,2,0:T(8,128)S(1)} async-done(((f32[16,128,256]{1,2,0:T(8,128)}), f32[16,128,256]{1,2,0:T(8,128)S(1)}, u32[]{:S(2)}, u32[]{:S(2)}) %all-to-all-start) | async-done | bytes 2097184 | tf_op jit(solution)/shard_map/while/body/eval_jaxpr/all_to_all | solution.py:52
  173.1 2.3 gather_fusion
  175.4 3.7 fusion.116
  182.4 7.1 %all-to-all-start = ((f32[16,128,256]{1,2,0:T(8,128)}), f32[16,128,256]{1,2,0:T(8,128)S(1)}, u32[]{:S(2)}, u32[]{:S(2)}) async-start(f32[16,128,256]{1,2,0:T(8,128)} %stack.3), calls=%async_computation | async-start | bytes 4194304 | tf_op jit(solution)/shard_map/while/body/eval_jaxpr/all_to_all | solution.py:52
  189.6 25.1 %all-to-all-done = f32[16,128,256]{1,2,0:T(8,128)S(1)} async-done(((f32[16,128,256]{1,2,0:T(8,128)}), f32[16,128,256]{1,2,0:T(8,128)S(1)}, u32[]{:S(2)}, u32[]{:S(2)}) %all-to-all-start) | async-done | bytes 2097184 | tf_op jit(solution)/shard_map/while/body/eval_jaxpr/all_to_all | solution.py:52
  216.5 2.3 gather_fusion
  218.8 3.7 fusion.116
  225.8 6.9 %all-to-all-start = ((f32[16,128,256]{1,2,0:T(8,128)}), f32[16,128,256]{1,2,0:T(8,128)S(1)}, u32[]{:S(2)}, u32[]{:S(2)}) async-start(f32[16,128,256]{1,2,0:T(8,128)} %stack.3), calls=%async_computation | async-start | bytes 4194304 | tf_op jit(solution)/shard_map/while/body/eval_jaxpr/all_to_all | solution.py:52
  232.8 25.0 %all-to-all-done = f32[16,128,256]{1,2,0:T(8,128)S(1)} async-done(((f32[16,128,256]{1,2,0:T(8,128)}), f32[16,128,256]{1,2,0:T(8,128)S(1)}, u32[]{:S(2)}, u32[]{:S(2)}) %all-to-all-start) | async-done | bytes 2097184 | tf_op jit(solution)/shard_map/while/body/eval_jaxpr/all_to_all | solution.py:52
  259.6 2.3 gather_fusion
  261.9 3.7 fusion.116
  268.9 7.1 %all-to-all-start = ((f32[16,128,256]{1,2,0:T(8,128)}), f32[16,128,256]{1,2,0:T(8,128)S(1)}, u32[]{:S(2)}, u32[]{:S(2)}) async-start(f32[16,128,256]{1,2,0:T(8,128)} %stack.3), calls=%async_computation | async-start | bytes 4194304 | tf_op jit(solution)/shard_map/while/body/eval_jaxpr/all_to_all | solution.py:52
  276.1 25.0 %all-to-all-done = f32[16,128,256]{1,2,0:T(8,128)S(1)} async-done(((f32[16,128,256]{1,2,0:T(8,128)}), f32[16,128,256]{1,2,0:T(8,128)S(1)}, u32[]{:S(2)}, u32[]{:S(2)}) %all-to-all-start) | async-done | bytes 2097184 | tf_op jit(solution)/shard_map/while/body/eval_jaxpr/all_to_all | solution.py:52
  303.0 2.3 gather_fusion
  305.2 3.7 fusion.116
  312.3 7.1 %all-to-all-start = ((f32[16,128,256]{1,2,0:T(8,128)}), f32[16,128,256]{1,2,0:T(8,128)S(1)}, u32[]{:S(2)}, u32[]{:S(2)}) async-start(f32[16,128,256]{1,2,0:T(8,128)} %stack.3), calls=%async_computation | async-start | bytes 4194304 | tf_op jit(solution)/shard_map/while/body/eval_jaxpr/all_to_all | solution.py:52
  319.5 25.1 %all-to-all-done = f32[16,128,256]{1,2,0:T(8,128)S(1)} async-done(((f32[16,128,256]{1,2,0:T(8,128)}), f32[16,128,256]{1,2,0:T(8,128)S(1)}, u32[]{:S(2)}, u32[]{:S(2)}) %all-to-all-start) | async-done | bytes 2097184 | tf_op jit(solution)/shard_map/while/body/eval_jaxpr/all_to_all | solution.py:52
  346.4 2.3 gather_fusion
  348.6 3.7 fusion.116
  353.1 2.4 reduce_sum.27
  355.5 5.6 fusion.7
  362.7 32.5 %psum.15 = f32[8,128]{1,0:T(8,128)S(1)} all-reduce(f32[8,128]{1,0:T(8,128)S(1)} %bitcast.129), channel_id=1, replica_groups=mesh['tm'=16,'row'=16] {'row'}, use_global_device_ids=true, to_apply=%region_6.7 | all-reduce | flops 1024 | bytes 8192 | tf_op jit(solution)/shard_map/psum | solution.py:75
  395.2 64.5 %all-reduce.2.cloned.1.call-done = f32[8,128,128]{2,1,0:T(8,128)} async-done(((f32[8,128,128]{2,1,0:T(8,128)}), f32[8,128,128]{2,1,0:T(8,128)}) %all-reduce.2.cloned.1.call-update) | async-done | bytes 524304 | tf_op jit(solution)/shard_map/psum | solution.py:75
  479.9 2.0 fusion.50
  481.9 2.0 while.40
  483.9 107.0 %while.41 = (s32[]{:T(128)}, f32[128,128]{1,0:T(8,128)S(1)}, pred[]{:T(512)}, f32[128,128]{1,0:T(8,128)S(1)}, s32[]{:T(128)}) while((s32[]{:T(128)}, f32[128,128]{1,0:T(8,128)S(1)}, pred[]{:T(512)}, f32[128,128]{1,0:T(8,128)S(1)}, s32[]{:T(128)}) %tuple.91), condition=%wide.region_11.12_spmd.clone, body=%wide.region_10.11_spmd.clone.sunk | while | flops 25214976 | bytes 589926 | solution.py:97
  484.2 3.9 collective-permute-start
  488.1 4.3 collective-permute-done
  492.6 1.9 collective-permute-start
  494.5 4.9 collective-permute-done
  499.6 1.9 collective-permute-start
  501.6 4.9 collective-permute-done
  506.7 1.9 collective-permute-start
  508.6 4.9 collective-permute-done
  513.7 1.9 collective-permute-start
  515.6 4.9 collective-permute-done
  520.8 1.9 collective-permute-start
  522.7 4.9 collective-permute-done
  529.7 4.9 collective-permute-done
  536.8 4.9 collective-permute-done
  543.8 4.9 collective-permute-done
  550.8 4.9 collective-permute-done
  557.9 4.9 collective-permute-done
  563.0 1.9 collective-permute-start
  564.9 4.9 collective-permute-done
  571.9 4.9 collective-permute-done
  579.0 4.9 collective-permute-done
  584.1 1.9 collective-permute-start
  586.0 4.9 collective-permute-done
  591.5 2.0 fusion.49
  (193 shorter events, 81.9 us)
Async XLA Ops:
  7.2 452.5 %all-reduce.2.cloned.1.call-start = ((), (), s32[]{:S(2)}) async-start(), calls=%async_computation.1 | async-start | bytes 1048576 | tf_op jit(solution)/shard_map/psum | solution.py:75
  9.8 6.9 %copy-start.6 = (s32[4,8]{1,0:T(4,128)S(1)}, s32[4,8]{1,0:T(4,128)}, u32[]{:S(2)}) copy-start(s32[4,8]{1,0:T(4,128)} %get-tuple-element.327) | copy-start | bytes 388 | tf_op jit(solution)/shard_map/while
  9.8 34.8 %all-to-all-start = ((f32[16,128,256]{1,2,0:T(8,128)}), f32[16,128,256]{1,2,0:T(8,128)S(1)}, u32[]{:S(2)}, u32[]{:S(2)}) async-start(f32[16,128,256]{1,2,0:T(8,128)} %stack.3), calls=%async_computation | async-start | bytes 4194304 | tf_op jit(solution)/shard_map/while/body/eval_jaxpr/all_to_all | solution.py:52
  55.6 4.1 copy-start.6
  55.6 29.2 %all-to-all-start = ((f32[16,128,256]{1,2,0:T(8,128)}), f32[16,128,256]{1,2,0:T(8,128)S(1)}, u32[]{:S(2)}, u32[]{:S(2)}) async-start(f32[16,128,256]{1,2,0:T(8,128)} %stack.3), calls=%async_computation | async-start | bytes 4194304 | tf_op jit(solution)/shard_map/while/body/eval_jaxpr/all_to_all | solution.py:52
  96.0 6.9 %copy-start.6 = (s32[4,8]{1,0:T(4,128)S(1)}, s32[4,8]{1,0:T(4,128)}, u32[]{:S(2)}) copy-start(s32[4,8]{1,0:T(4,128)} %get-tuple-element.327) | copy-start | bytes 388 | tf_op jit(solution)/shard_map/while
  96.0 32.0 %all-to-all-start = ((f32[16,128,256]{1,2,0:T(8,128)}), f32[16,128,256]{1,2,0:T(8,128)S(1)}, u32[]{:S(2)}, u32[]{:S(2)}) async-start(f32[16,128,256]{1,2,0:T(8,128)} %stack.3), calls=%async_computation | async-start | bytes 4194304 | tf_op jit(solution)/shard_map/while/body/eval_jaxpr/all_to_all | solution.py:52
  139.0 7.1 %copy-start.6 = (s32[4,8]{1,0:T(4,128)S(1)}, s32[4,8]{1,0:T(4,128)}, u32[]{:S(2)}) copy-start(s32[4,8]{1,0:T(4,128)} %get-tuple-element.327) | copy-start | bytes 388 | tf_op jit(solution)/shard_map/while
  139.0 32.2 %all-to-all-start = ((f32[16,128,256]{1,2,0:T(8,128)}), f32[16,128,256]{1,2,0:T(8,128)S(1)}, u32[]{:S(2)}, u32[]{:S(2)}) async-start(f32[16,128,256]{1,2,0:T(8,128)} %stack.3), calls=%async_computation | async-start | bytes 4194304 | tf_op jit(solution)/shard_map/while/body/eval_jaxpr/all_to_all | solution.py:52
  182.4 7.1 %copy-start.6 = (s32[4,8]{1,0:T(4,128)S(1)}, s32[4,8]{1,0:T(4,128)}, u32[]{:S(2)}) copy-start(s32[4,8]{1,0:T(4,128)} %get-tuple-element.327) | copy-start | bytes 388 | tf_op jit(solution)/shard_map/while
  182.4 32.3 %all-to-all-start = ((f32[16,128,256]{1,2,0:T(8,128)}), f32[16,128,256]{1,2,0:T(8,128)S(1)}, u32[]{:S(2)}, u32[]{:S(2)}) async-start(f32[16,128,256]{1,2,0:T(8,128)} %stack.3), calls=%async_computation | async-start | bytes 4194304 | tf_op jit(solution)/shard_map/while/body/eval_jaxpr/all_to_all | solution.py:52
  225.8 6.9 %copy-start.6 = (s32[4,8]{1,0:T(4,128)S(1)}, s32[4,8]{1,0:T(4,128)}, u32[]{:S(2)}) copy-start(s32[4,8]{1,0:T(4,128)} %get-tuple-element.327) | copy-start | bytes 388 | tf_op jit(solution)/shard_map/while
  225.8 32.0 %all-to-all-start = ((f32[16,128,256]{1,2,0:T(8,128)}), f32[16,128,256]{1,2,0:T(8,128)S(1)}, u32[]{:S(2)}, u32[]{:S(2)}) async-start(f32[16,128,256]{1,2,0:T(8,128)} %stack.3), calls=%async_computation | async-start | bytes 4194304 | tf_op jit(solution)/shard_map/while/body/eval_jaxpr/all_to_all | solution.py:52
  268.9 7.1 %copy-start.6 = (s32[4,8]{1,0:T(4,128)S(1)}, s32[4,8]{1,0:T(4,128)}, u32[]{:S(2)}) copy-start(s32[4,8]{1,0:T(4,128)} %get-tuple-element.327) | copy-start | bytes 388 | tf_op jit(solution)/shard_map/while
  268.9 32.2 %all-to-all-start = ((f32[16,128,256]{1,2,0:T(8,128)}), f32[16,128,256]{1,2,0:T(8,128)S(1)}, u32[]{:S(2)}, u32[]{:S(2)}) async-start(f32[16,128,256]{1,2,0:T(8,128)} %stack.3), calls=%async_computation | async-start | bytes 4194304 | tf_op jit(solution)/shard_map/while/body/eval_jaxpr/all_to_all | solution.py:52
  312.2 7.1 %copy-start.6 = (s32[4,8]{1,0:T(4,128)S(1)}, s32[4,8]{1,0:T(4,128)}, u32[]{:S(2)}) copy-start(s32[4,8]{1,0:T(4,128)} %get-tuple-element.327) | copy-start | bytes 388 | tf_op jit(solution)/shard_map/while
  312.3 32.3 %all-to-all-start = ((f32[16,128,256]{1,2,0:T(8,128)}), f32[16,128,256]{1,2,0:T(8,128)S(1)}, u32[]{:S(2)}, u32[]{:S(2)}) async-start(f32[16,128,256]{1,2,0:T(8,128)} %stack.3), calls=%async_computation | async-start | bytes 4194304 | tf_op jit(solution)/shard_map/while/body/eval_jaxpr/all_to_all | solution.py:52
  353.1 2.4 copy-start.7
  353.1 2.4 copy-start.8
  353.1 2.4 copy-start
  361.2 102.3 %copy-start.2 = (f32[128,128]{1,0:T(8,128)}, f32[128,128]{1,0:T(8,128)S(1)}, u32[]{:S(2)}) copy-start(f32[128,128]{1,0:T(8,128)S(1)} %fusion.29) | copy-start | bytes 196612
  459.7 3.8 copy-start.5
  476.2 3.2 copy-start.9
  476.8 3.0 copy-start.1
  479.6 2.3 copy-start.4
  479.9 4.1 copy-start.3
  484.2 8.2 %collective-permute-start = (f32[128,128]{1,0:T(8,128)S(1)}, f32[128,128]{1,0:T(8,128)S(1)}, u32[]{:S(2)}, u32[]{:S(2)}) collective-permute-start(f32[128,128]{1,0:T(8,128)S(1)} %fusion.120), channel_id=1, source_target_pairs={{16,0},{32,16},{48,32},{64,48},{80,64},{96,80},{112,96},{128,112},... | collective-permute-start | bytes 196616 | tf_op jit(solution)/shard_map/while/body/eval_jaxpr/ppermute | solution.py:13
  492.6 6.8 %collective-permute-start = (f32[128,128]{1,0:T(8,128)S(1)}, f32[128,128]{1,0:T(8,128)S(1)}, u32[]{:S(2)}, u32[]{:S(2)}) collective-permute-start(f32[128,128]{1,0:T(8,128)S(1)} %fusion.120), channel_id=1, source_target_pairs={{16,0},{32,16},{48,32},{64,48},{80,64},{96,80},{112,96},{128,112},... | collective-permute-start | bytes 196616 | tf_op jit(solution)/shard_map/while/body/eval_jaxpr/ppermute | solution.py:13
  499.6 6.8 %collective-permute-start = (f32[128,128]{1,0:T(8,128)S(1)}, f32[128,128]{1,0:T(8,128)S(1)}, u32[]{:S(2)}, u32[]{:S(2)}) collective-permute-start(f32[128,128]{1,0:T(8,128)S(1)} %fusion.120), channel_id=1, source_target_pairs={{16,0},{32,16},{48,32},{64,48},{80,64},{96,80},{112,96},{128,112},... | collective-permute-start | bytes 196616 | tf_op jit(solution)/shard_map/while/body/eval_jaxpr/ppermute | solution.py:13
  506.7 6.8 %collective-permute-start = (f32[128,128]{1,0:T(8,128)S(1)}, f32[128,128]{1,0:T(8,128)S(1)}, u32[]{:S(2)}, u32[]{:S(2)}) collective-permute-start(f32[128,128]{1,0:T(8,128)S(1)} %fusion.120), channel_id=1, source_target_pairs={{16,0},{32,16},{48,32},{64,48},{80,64},{96,80},{112,96},{128,112},... | collective-permute-start | bytes 196616 | tf_op jit(solution)/shard_map/while/body/eval_jaxpr/ppermute | solution.py:13
  513.7 6.8 %collective-permute-start = (f32[128,128]{1,0:T(8,128)S(1)}, f32[128,128]{1,0:T(8,128)S(1)}, u32[]{:S(2)}, u32[]{:S(2)}) collective-permute-start(f32[128,128]{1,0:T(8,128)S(1)} %fusion.120), channel_id=1, source_target_pairs={{16,0},{32,16},{48,32},{64,48},{80,64},{96,80},{112,96},{128,112},... | collective-permute-start | bytes 196616 | tf_op jit(solution)/shard_map/while/body/eval_jaxpr/ppermute | solution.py:13
  520.8 6.8 %collective-permute-start = (f32[128,128]{1,0:T(8,128)S(1)}, f32[128,128]{1,0:T(8,128)S(1)}, u32[]{:S(2)}, u32[]{:S(2)}) collective-permute-start(f32[128,128]{1,0:T(8,128)S(1)} %fusion.120), channel_id=1, source_target_pairs={{16,0},{32,16},{48,32},{64,48},{80,64},{96,80},{112,96},{128,112},... | collective-permute-start | bytes 196616 | tf_op jit(solution)/shard_map/while/body/eval_jaxpr/ppermute | solution.py:13
  527.8 6.8 %collective-permute-start = (f32[128,128]{1,0:T(8,128)S(1)}, f32[128,128]{1,0:T(8,128)S(1)}, u32[]{:S(2)}, u32[]{:S(2)}) collective-permute-start(f32[128,128]{1,0:T(8,128)S(1)} %fusion.120), channel_id=1, source_target_pairs={{16,0},{32,16},{48,32},{64,48},{80,64},{96,80},{112,96},{128,112},... | collective-permute-start | bytes 196616 | tf_op jit(solution)/shard_map/while/body/eval_jaxpr/ppermute | solution.py:13
  534.8 6.8 %collective-permute-start = (f32[128,128]{1,0:T(8,128)S(1)}, f32[128,128]{1,0:T(8,128)S(1)}, u32[]{:S(2)}, u32[]{:S(2)}) collective-permute-start(f32[128,128]{1,0:T(8,128)S(1)} %fusion.120), channel_id=1, source_target_pairs={{16,0},{32,16},{48,32},{64,48},{80,64},{96,80},{112,96},{128,112},... | collective-permute-start | bytes 196616 | tf_op jit(solution)/shard_map/while/body/eval_jaxpr/ppermute | solution.py:13
  541.9 6.8 %collective-permute-start = (f32[128,128]{1,0:T(8,128)S(1)}, f32[128,128]{1,0:T(8,128)S(1)}, u32[]{:S(2)}, u32[]{:S(2)}) collective-permute-start(f32[128,128]{1,0:T(8,128)S(1)} %fusion.120), channel_id=1, source_target_pairs={{16,0},{32,16},{48,32},{64,48},{80,64},{96,80},{112,96},{128,112},... | collective-permute-start | bytes 196616 | tf_op jit(solution)/shard_map/while/body/eval_jaxpr/ppermute | solution.py:13
  548.9 6.8 %collective-permute-start = (f32[128,128]{1,0:T(8,128)S(1)}, f32[128,128]{1,0:T(8,128)S(1)}, u32[]{:S(2)}, u32[]{:S(2)}) collective-permute-start(f32[128,128]{1,0:T(8,128)S(1)} %fusion.120), channel_id=1, source_target_pairs={{16,0},{32,16},{48,32},{64,48},{80,64},{96,80},{112,96},{128,112},... | collective-permute-start | bytes 196616 | tf_op jit(solution)/shard_map/while/body/eval_jaxpr/ppermute | solution.py:13
  555.9 6.8 %collective-permute-start = (f32[128,128]{1,0:T(8,128)S(1)}, f32[128,128]{1,0:T(8,128)S(1)}, u32[]{:S(2)}, u32[]{:S(2)}) collective-permute-start(f32[128,128]{1,0:T(8,128)S(1)} %fusion.120), channel_id=1, source_target_pairs={{16,0},{32,16},{48,32},{64,48},{80,64},{96,80},{112,96},{128,112},... | collective-permute-start | bytes 196616 | tf_op jit(solution)/shard_map/while/body/eval_jaxpr/ppermute | solution.py:13
  563.0 6.8 %collective-permute-start = (f32[128,128]{1,0:T(8,128)S(1)}, f32[128,128]{1,0:T(8,128)S(1)}, u32[]{:S(2)}, u32[]{:S(2)}) collective-permute-start(f32[128,128]{1,0:T(8,128)S(1)} %fusion.120), channel_id=1, source_target_pairs={{16,0},{32,16},{48,32},{64,48},{80,64},{96,80},{112,96},{128,112},... | collective-permute-start | bytes 196616 | tf_op jit(solution)/shard_map/while/body/eval_jaxpr/ppermute | solution.py:13
  570.0 6.8 %collective-permute-start = (f32[128,128]{1,0:T(8,128)S(1)}, f32[128,128]{1,0:T(8,128)S(1)}, u32[]{:S(2)}, u32[]{:S(2)}) collective-permute-start(f32[128,128]{1,0:T(8,128)S(1)} %fusion.120), channel_id=1, source_target_pairs={{16,0},{32,16},{48,32},{64,48},{80,64},{96,80},{112,96},{128,112},... | collective-permute-start | bytes 196616 | tf_op jit(solution)/shard_map/while/body/eval_jaxpr/ppermute | solution.py:13
  577.1 6.8 %collective-permute-start = (f32[128,128]{1,0:T(8,128)S(1)}, f32[128,128]{1,0:T(8,128)S(1)}, u32[]{:S(2)}, u32[]{:S(2)}) collective-permute-start(f32[128,128]{1,0:T(8,128)S(1)} %fusion.120), channel_id=1, source_target_pairs={{16,0},{32,16},{48,32},{64,48},{80,64},{96,80},{112,96},{128,112},... | collective-permute-start | bytes 196616 | tf_op jit(solution)/shard_map/while/body/eval_jaxpr/ppermute | solution.py:13
  584.1 6.8 %collective-permute-start = (f32[128,128]{1,0:T(8,128)S(1)}, f32[128,128]{1,0:T(8,128)S(1)}, u32[]{:S(2)}, u32[]{:S(2)}) collective-permute-start(f32[128,128]{1,0:T(8,128)S(1)} %fusion.120), channel_id=1, source_target_pairs={{16,0},{32,16},{48,32},{64,48},{80,64},{96,80},{112,96},{128,112},... | collective-permute-start | bytes 196616 | tf_op jit(solution)/shard_map/while/body/eval_jaxpr/ppermute | solution.py:13
Sparse Core Ops, SparseCore 0:
  361.3 98.3 all-reduce.1
